TPU v7x, 256 devices: a whole 4x4x8 slice. The times are simulated.
256 devices in a mesh: rows: 64 (over z, x, core), rep: 4 (over y).
Axes of the slice: x: 4, y: 4, z: 8, core: 2. Of those that a mesh axis runs over, the one named last changes fastest.
Arguments:
- embeddings: bfloat16 [262144, 1024], P(('rows', 'rep')), may hold values from -0.25 to 0.25
- assignments: int32 [262144], P(('rows', 'rep')), may hold values from 0 to 65535, as said below
- old_centroids: bfloat16 [65536, 1024], P('rows'), may hold values from -0.25 to 0.25
- prior_counts: int32 [65536], P('rows'), may hold values from 1 to 8
Outputs:
- centroids: bfloat16 [65536, 1024], P('rows')
- row_score: float32 [262144], P(('rows', 'rep'))
Inputs may be any that keep to these rules, and one draw needn't show every extreme that they name: Within each device's aligned block of 1024 rows the assignments never fall. Cluster k belongs to owner k // 1024; in every block at most 32 rows belong to one owner, and some owner receives exactly 32 of them.
All inputs are finite; a program needn't handle non-finite values.
Results may differ from a plain program's by a relative error of at most 0.0028.
Values may be sent and summed in bfloat16 or wider, within the bound.
A program may use at most 64 MiB of HBM per device.

v0:
```python
import jax
import jax.numpy as jnp
from jax import lax
from jax.sharding import PartitionSpec as P


def finalize(sums, counts, old_block, prior_block):
    prior = prior_block.astype(jnp.float32)
    total = prior + counts
    mean = (prior[:, None] * old_block.astype(jnp.float32) + sums) / total[:, None]
    scale = lax.rsqrt(jnp.sum(mean * mean, axis=1, keepdims=True) + 1e-06)
    return ((mean * scale).astype(jnp.bfloat16), (1.0 / total).astype(jnp.bfloat16))


def on_device(embeddings, assignments, old_centroids, prior_counts):
    rows_here = embeddings.shape[0]
    width = embeddings.shape[1]
    owners = lax.axis_size("rows")
    per_owner = old_centroids.shape[0]
    capacity = 2 * rows_here // owners
    owner_of = assignments // per_owner
    owner_list = jnp.arange(owners, dtype=jnp.int32)
    bounds = owner_list * per_owner
    starts = jnp.sum((assignments[None, :] < bounds[:, None]).astype(jnp.int32), axis=1)
    loads = jnp.sum((owner_of[None, :] == owner_list[:, None]).astype(jnp.int32), axis=1)
    position = jnp.arange(capacity, dtype=jnp.int32)
    source = jnp.clip(starts[:, None] + position[None, :], 0, rows_here - 1)
    live = position[None, :] < loads[:, None]
    outgoing = jnp.where(live[:, :, None], embeddings[source], jnp.zeros((), jnp.bfloat16))
    local_ids = jnp.where(live, assignments[source] - bounds[:, None], -1)
    arrived, arrived_ids = (
        lax.all_to_all(outgoing, "rows", split_axis=0, concat_axis=0, tiled=True),
        lax.all_to_all(local_ids, "rows", split_axis=0, concat_axis=0, tiled=True),
    )
    flat = arrived.reshape(-1, width)
    flat_ids = arrived_ids.reshape(-1)
    onehot = (flat_ids[:, None] == jnp.arange(per_owner, dtype=jnp.int32)[None, :]).astype(
        jnp.bfloat16
    )
    partial_sums = lax.dot_general(
        onehot, flat, (((0,), (0,)), ((), ())), preferred_element_type=jnp.float32
    )
    tally = jnp.sum(onehot, axis=0, dtype=jnp.float32)
    sums, counts = lax.psum((partial_sums, tally), "rep")
    centroids, weight = finalize(sums, counts, old_centroids, prior_counts)
    slot_of = jnp.arange(rows_here, dtype=jnp.int32) - starts[owner_of]
    safe_ids = jnp.clip(arrived_ids, 0, per_owner - 1)
    flat_safe = safe_ids.reshape(-1)
    near = centroids[flat_safe].astype(jnp.float32)
    diff = flat.astype(jnp.float32) - near
    dist = jnp.sum(diff * diff, axis=1)
    slot_scores = (weight[flat_safe].astype(jnp.float32) * dist).reshape(owners, capacity)
    returned = lax.all_to_all(slot_scores, "rows", split_axis=0, concat_axis=0, tiled=True)
    row_score = returned[owner_of, slot_of]
    return (centroids, row_score)


def solution(mesh):
    placed = (P(("rows", "rep"), None), P(("rows", "rep")), P("rows", None), P("rows"))
    return jax.shard_map(
        on_device,
        mesh=mesh,
        in_specs=placed,
        out_specs=(P("rows", None), P(("rows", "rep"))),
        check_vma=False,
    )
```

profile of v0, /device:TPU:1, one launch (start us, length us, event | category | flops | bytes accessed | tf_op | source)
XLA Modules:
  0.0 316.8 jit_solution(5519018296415916002)
XLA Ops:
  7.2 0.0 copy-start
  7.2 0.0 copy-start.1
  7.2 0.8 clamp_shift-left_fusion
  8.0 0.9 convert_reduce_fusion.1
  8.9 0.1 compare_select_fusion
  9.0 0.1 reshape.220
  9.1 0.0 copy-done.1
  9.1 8.6 %gather_fusion = s32[2048]{0:T(1024)S(1)} fusion(s32[1024]{0:T(1024)S(1)} %copy-done.1, s32[2048]{0:T(1024)S(1)} %broadcast_clamp_fusion.1), kind=kCustom, calls=%fused_computation | custom fusion | bytes 24576 | tf_op jit(solution)/shard_map/gather | solution.py:30
  17.7 0.1 gather.23
  17.8 0.1 convert_reduce_fusion.2
  17.9 0.7 subtract_select_fusion
  18.6 13.0 %all-to-all-start = ((s32[64,1,32]{2,1,0:T(1,128)}), s32[64,1,32]{2,1,0:T(1,128)S(1)}, u32[]{:S(2)}, u32[]{:S(2)}) async-start(s32[64,1,32]{2,1,0:T(1,128)} %bitcast), calls=%async_computation | async-start | bytes 65536 | tf_op jit(solution)/shard_map/all_to_all | solution.py:33
  31.6 0.1 iota_compare_fusion.3
  31.7 0.0 copy-done
  31.7 9.7 %gather_fusion.1 = bf16[2048,1024]{1,0:T(8,128)(2,1)} fusion(bf16[1024,1024]{1,0:T(8,128)(2,1)S(1)} %copy-done, s32[2048]{0:T(1024)S(1)} %broadcast_clamp_fusion.1), kind=kCustom, calls=%fused_computation.1 | custom fusion | bytes 8396800 | tf_op jit(solution)/shard_map/gather | solution.py:29
  41.4 3.8 %broadcast_select_fusion = bf16[64,32,1024]{2,1,0:T(8,128)(2,1)} fusion(bf16[64,32,1024]{2,1,0:T(8,128)(2,1)} %bitcast.83, pred[64,32]{1,0:T(8,128)(4,1)S(1)} %iota_compare_fusion.3), kind=kLoop, calls=%fused_computation.16 | loop fusion | flops 2097152 | bytes 8390656 | tf_op jit(solution)/shard_map/jit(_where)/select_n | solution.py:29
  45.2 0.0 all-to-all-done
  45.2 10.5 %all-to-all-start.1 = ((bf16[64,32,1024]{2,1,0:T(8,128)(2,1)}), bf16[64,32,1024]{2,1,0:T(8,128)(2,1)}, u32[]{:S(2)}, u32[]{:S(2)}) async-start(bf16[64,32,1024]{2,1,0:T(8,128)(2,1)} %broadcast_select_fusion), calls=%async_computation.1 | async-start | bytes 8388608 | tf_op jit(solution)/shard_map/all_to_all | solution.py:32
  55.6 0.0 all-reduce.2.cloned.1.call-start
  55.7 0.5 broadcast.497
  56.2 0.8 clamp_reduce_fusion
  57.1 0.1 eq.31
  57.1 92.9 %all-to-all-done.1 = bf16[64,32,1024]{2,1,0:T(8,128)(2,1)} async-done(((bf16[64,32,1024]{2,1,0:T(8,128)(2,1)}), bf16[64,32,1024]{2,1,0:T(8,128)(2,1)}, u32[]{:S(2)}, u32[]{:S(2)}) %all-to-all-start.1) | async-done | bytes 4194336 | tf_op jit(solution)/shard_map/all_to_all | solution.py:32
  150.1 8.8 %fusion.3 = f32[1024,1024]{1,0:T(8,128)} fusion(bf16[2048,1024]{1,0:T(8,128)(2,1)} %bitcast.2, s32[2048]{0:T(1024)S(1)} %eq.31), kind=kOutput, calls=%fused_computation.11 | convolution fusion | flops 4297064448 | bytes 8396800 | tf_op jit(solution)/shard_map/dot_general | solution.py:40
  158.9 0.0 copy-start.2
  158.9 0.0 all-reduce.2.cloned.1.call-update
  158.9 0.7 copy-done.2
  159.5 0.7 fusion.13
  160.2 0.7 fusion.10
  160.9 0.7 fusion.11
  161.6 0.7 fusion.12
  162.4 39.7 %select_select_fusion = s32[1024]{0:T(1024)S(1)} fusion(s32[]{:T(128)} %bitcast.9, s32[]{:T(128)} %bitcast.10, s32[]{:T(128)} %bitcast.11, s32[]{:T(128)} %bitcast.12, s32[]{:T(128)} %bitcast.13, s32[]{:T(128)} %bitcast.14, s32[]{:T(128)} %bitcast.15, s32[]{:T(128)} %bitcast.16, s32[]{:T(128)} %bitcast.17, s32[]{:T(128)} %bitcast.18, s32[]{:T(128)} %bitcast.19, ...), kind=kLoop, calls=%fused_computation.40 | loop fusion | flops 147456 | bytes 8448 | tf_op jit(solution)/shard_map/gather | solution.py:46
  202.1 0.1 min.20
  202.2 1.0 convert_reduce_fusion
  203.2 8.7 %psum.15 = f32[1024]{0:T(1024)S(1)} all-reduce(f32[1024]{0:T(1024)S(1)} %convert_reduce_fusion), channel_id=1, replica_groups=mesh['rows'=64,'rep'=4] {'rep'}, use_global_device_ids=true, to_apply=%region_4.5 | all-reduce | flops 1024 | bytes 8192 | tf_op jit(solution)/shard_map/psum | solution.py:44
  212.0 13.1 %gather_fusion.2 = bf16[2048]{0:T(1024)(128)(2,1)S(1)} fusion(bf16[1024]{0:T(1024)(128)(2,1)S(1)} %get-tuple-element.4, s32[2048]{0:T(1024)S(1)} %broadcast_clamp_fusion), kind=kCustom, calls=%fused_computation.2 | custom fusion | bytes 16384 | tf_op jit(solution)/shard_map/gather | solution.py:52
  225.1 0.1 reshape.216
  225.1 29.9 %all-reduce.2.cloned.1.call-done = f32[1024,1024]{1,0:T(8,128)} async-done(((f32[1024,1024]{1,0:T(8,128)}), f32[1024,1024]{1,0:T(8,128)}) %all-reduce.2.cloned.1.call-update) | async-done | bytes 4194320 | tf_op jit(solution)/shard_map/psum | solution.py:44
  255.1 3.5 %multiply_reduce_fusion = (f32[1024]{0:T(1024)S(1)}, f32[1024,1024]{1,0:T(8,128)S(1)}) fusion(f32[1024]{0:T(1024)S(1)} %get-tuple-element.5, f32[1024,1024]{1,0:T(8,128)} %all-reduce.2.cloned.1.call-done, bf16[1024,1024]{1,0:T(8,128)(2,1)} %param.6, f32[1024]{0:T(1024)S(1)} %convert_element_type.49), kind=kLoop, calls=%fused_computation.13 | loop fusion | flops 6290432 | bytes 10498048 | tf_op jit(solution)/shard_map/reduce_sum | solution.py:11
  258.6 1.6 multiply_convert_fusion
  260.2 12.8 %gather_fusion.3 = bf16[2048,1024]{1,0:T(8,128)(2,1)} fusion(bf16[1024,1024]{1,0:T(8,128)(2,1)} %multiply_convert_fusion, s32[2048]{0:T(1024)S(1)} %broadcast_clamp_fusion), kind=kCustom, calls=%fused_computation.3 | custom fusion | bytes 8396800 | tf_op jit(solution)/shard_map/gather | solution.py:49
  273.0 4.9 %fusion.1 = f32[64,32]{1,0:T(8,128)S(1)} fusion(bf16[64,32,1024]{2,1,0:T(8,128)(2,1)} %bitcast.82, bf16[64,32,1024]{2,1,0:T(8,128)(2,1)} %all-to-all-done.1), kind=kLoop, calls=%fused_computation.7 | loop fusion | flops 10483712 | bytes 8396800 | tf_op jit(solution)/shard_map/reduce_sum | solution.py:51
  277.9 0.6 bitcast_multiply_fusion
  278.5 10.7 %all-to-all-start.2 = ((f32[64,1,32]{2,1,0:T(1,128)}), f32[64,1,32]{2,1,0:T(1,128)S(1)}, u32[]{:S(2)}, u32[]{:S(2)}) async-start(f32[64,1,32]{2,1,0:T(1,128)} %bitcast.6), calls=%async_computation.2 | async-start | bytes 65536 | tf_op jit(solution)/shard_map/all_to_all | solution.py:53
  289.2 9.3 %all-to-all-done.2 = f32[64,1,32]{2,1,0:T(1,128)S(1)} async-done(((f32[64,1,32]{2,1,0:T(1,128)}), f32[64,1,32]{2,1,0:T(1,128)S(1)}, u32[]{:S(2)}, u32[]{:S(2)}) %all-to-all-start.2) | async-done | bytes 8224 | tf_op jit(solution)/shard_map/all_to_all | solution.py:53
  298.5 11.5 %gather_fusion.4 = f32[1024]{0:T(1024)} fusion(f32[64,32]{1,0:T(8,128)S(1)} %bitcast.80, s32[1024]{0:T(1024)S(1)} %bitcast.81), kind=kCustom, calls=%fused_computation.4 | custom fusion | bytes 16384 | tf_op jit(solution)/shard_map/gather | solution.py:54
  (8 shorter events, 0.1 us)
Async XLA Ops:
  7.2 24.5 %copy-start = (bf16[1024,1024]{1,0:T(8,128)(2,1)S(1)}, bf16[1024,1024]{1,0:T(8,128)(2,1)}, u32[]{:S(2)}) copy-start(bf16[1024,1024]{1,0:T(8,128)(2,1)} %param.4) | copy-start | bytes 6291460
  7.2 1.9 copy-start.1
  18.6 26.5 %all-to-all-start = ((s32[64,1,32]{2,1,0:T(1,128)}), s32[64,1,32]{2,1,0:T(1,128)S(1)}, u32[]{:S(2)}, u32[]{:S(2)}) async-start(s32[64,1,32]{2,1,0:T(1,128)} %bitcast), calls=%async_computation | async-start | bytes 65536 | tf_op jit(solution)/shard_map/all_to_all | solution.py:33
  45.2 104.9 %all-to-all-start.1 = ((bf16[64,32,1024]{2,1,0:T(8,128)(2,1)}), bf16[64,32,1024]{2,1,0:T(8,128)(2,1)}, u32[]{:S(2)}, u32[]{:S(2)}) async-start(bf16[64,32,1024]{2,1,0:T(8,128)(2,1)} %broadcast_select_fusion), calls=%async_computation.1 | async-start | bytes 8388608 | tf_op jit(solution)/shard_map/all_to_all | solution.py:32
  55.6 199.4 %all-reduce.2.cloned.1.call-start = ((), (), s32[]{:S(2)}) async-start(), calls=%async_computation.3 | async-start | bytes 8388608 | tf_op jit(solution)/shard_map/psum | solution.py:44
  158.9 0.7 copy-start.2
  278.5 20.0 %all-to-all-start.2 = ((f32[64,1,32]{2,1,0:T(1,128)}), f32[64,1,32]{2,1,0:T(1,128)S(1)}, u32[]{:S(2)}, u32[]{:S(2)}) async-start(f32[64,1,32]{2,1,0:T(1,128)} %bitcast.6), calls=%async_computation.2 | async-start | bytes 65536 | tf_op jit(solution)/shard_map/all_to_all | solution.py:53
Sparse Core Ops, SparseCore 0:
  159.0 96.0 all-reduce.1
where the time goes:
time: 318 us; the launch traced here: 317 us
  waiting for transfers between devices  132 us (42%)
  local copies, waits for them, and re-layouts  60 us (19%)
  other arithmetic  58.7 us (18%)
  starting transfers between devices  34.2 us (11%)
  between operations  14.2 us (4%)
  matrix products  8.8 us (3%)
  blocking collectives  8.73 us (3%)
    all_to_all x1, waiting for transfers between devices, on_device(): lax.all_to_all(outgoing, 'rows', split_axis=0, concat_axis=0, tiled=True)  92.9 us
    gather x1, other arithmetic, on_device(): slot_of = jnp.arange(rows_here, dtype=jnp.int32) - starts[owner_of]  39.7 us
    psum x1, waiting for transfers between devices, on_device(): sums, counts = lax.psum((partial_sums, tally), 'rep')  29.9 us
    gather x1, local copies, waits for them, and re-layouts, on_device(): weight[flat_safe].astype(jnp.float32) * dist  13.1 us
    all_to_all x1, starting transfers between devices, on_device(): lax.all_to_all(local_ids, 'rows', split_axis=0, concat_axis=0, tiled=True)  13 us
    gather x1, local copies, waits for them, and re-layouts, on_device(): near = centroids[flat_safe].astype(jnp.float32)  12.8 us
    gather x1, local copies, waits for them, and re-layouts, on_device(): row_score = returned[owner_of, slot_of]  11.5 us
    all_to_all x1, starting transfers between devices, on_device(): lax.all_to_all(slot_scores, 'rows', split_axis=0, concat_axis=0, tiled=True)  10.7 us
  transfers between devices with their start and end apart: 4, of which 3 were waited for; matrix products, arithmetic and copies ran while one was open for 23% of the time, Pallas kernels for 0%

commit v1 on v0

v1 whole, which is shorter than its diff:
```python
import functools

import jax
import jax.numpy as jnp
from jax import lax
from jax.experimental import pallas as pl
from jax.experimental.pallas import tpu as pltpu
from jax.sharding import PartitionSpec as P

MESH = pl.DeviceIdType.MESH
F32, BF16, I32 = jnp.float32, jnp.bfloat16, jnp.int32
LANES = 128
NT = (((1,), (1,)), ((), ()))
TN = (((0,), (0,)), ((), ()))


def displacements(planes, columns):
    z_order = []
    for step in range(planes // 2, 0, -1):
        z_order += [step, planes - step] if step != planes - step else [step]
    half = len(z_order) // 2
    z_order = [z for pair in zip(z_order[:half], z_order[half:]) for z in pair] + z_order[2 * half :]
    z_order.append(0)
    order = [
        (z_order[i % planes], (i // planes + i) % columns, (i // (planes * columns) + i) % 2)
        for i in range(planes * columns * 2)
    ]
    assert len(set(order)) == planes * columns * 2
    return [one for one in order if one != (0, 0, 0)]


def bf(mask):
    return jnp.where(mask, 1.0, 0.0).astype(BF16)


def kernel(
    owners, copies, cap, chunks,
    emb_ref, assign_ref, old_ref, prior_ref,
    cent_ref, score_ref,
    out, arr, pick, pick_t, part, rs_in, mean, acc, old, total_b, prior_b, weight_b, sumsq,
    ids_out, ids_in, cnt, sc_out, sc_in,
    send_sem, recv_sem, ids_sem, cnt_sem, rs_sem, ag_sem, sc_sem, old_sem,
):
    rows_here, width = emb_ref.shape
    per_owner = old_ref.shape[0]
    slots = owners * cap
    wide = width // chunks
    quarter = per_owner // copies
    me, rep = lax.axis_index("rows"), lax.axis_index("rep")
    columns = 4
    planes = owners // (2 * columns)
    z, x, core = me // (2 * columns), (me // 2) % columns, me % 2
    peers = [
        ((z + dz) % planes) * (2 * columns) + ((x + dx) % columns) * 2 + (core + dc) % 2
        for dz, dx, dc in displacements(planes, columns)
    ]
    mates = [lax.rem(rep + d, copies) for d in range(1, copies)]

    old_copy = pltpu.make_async_copy(old_ref, old, old_sem)
    old_copy.start()

    barrier = pltpu.get_barrier_semaphore()
    for peer in peers:
        pl.semaphore_signal(barrier, inc=1, device_id={"rows": peer}, device_id_type=MESH)
    for mate in mates:
        pl.semaphore_signal(barrier, inc=1, device_id={"rep": mate}, device_id_type=MESH)

    assign = assign_ref[...]
    owner_row = assign // per_owner
    local_row = assign - owner_row * per_owner
    owner_col = lax.broadcasted_iota(I32, (owners, rows_here), 0)
    mine = owner_row == owner_col
    starts = jnp.sum(jnp.where(owner_row < owner_col, 1.0, 0.0), axis=1, keepdims=True)
    start_row = jnp.sum(jnp.where(mine, starts, 0.0), axis=0, keepdims=True).astype(I32)
    rank_row = lax.broadcasted_iota(I32, (1, rows_here), 1) - start_row
    slot_row = owner_row * cap + rank_row

    code = local_row + 1
    at_rank = lax.broadcasted_iota(I32, (LANES, rows_here), 0) == rank_row
    high = jnp.where(at_rank, code // 32, 0).astype(F32).astype(BF16)
    low = jnp.where(at_rank, code % 32, 0).astype(F32).astype(BF16)
    mine_b = bf(mine)
    code_out = 32.0 * lax.dot_general(mine_b, high, NT, preferred_element_type=F32)
    code_out += lax.dot_general(mine_b, low, NT, preferred_element_type=F32)
    ids_out[...] = code_out.astype(I32).reshape(owners, 1, LANES)

    block = 256
    for b in range(slots // block):
        s = lax.broadcasted_iota(I32, (block, rows_here), 0) + b * block
        pick[b * block : (b + 1) * block, :] = bf(s == slot_row)

    pl.semaphore_wait(barrier, len(peers) + len(mates))

    ids_in[pl.ds(me, 1)] = ids_out[pl.ds(me, 1)]
    for peer in peers:
        pltpu.make_async_remote_copy(
            src_ref=ids_out.at[pl.ds(peer, 1)],
            dst_ref=ids_in.at[pl.ds(me, 1)],
            send_sem=ids_sem.at[0],
            recv_sem=ids_sem.at[1],
            device_id={"rows": peer},
            device_id_type=MESH,
        ).start()

    def fill(c):
        cols = pl.ds(pl.multiple_of(c * wide, wide), wide)
        out[c] = jnp.dot(pick[...], emb_ref[:, cols], preferred_element_type=F32).astype(BF16)
        here = pl.ds(pl.multiple_of(me * cap, cap), cap)
        arr[c, here, :] = out[c, here, :]

    def send(c):
        for peer in peers:
            pltpu.make_async_remote_copy(
                src_ref=out.at[c, pl.ds(pl.multiple_of(peer * cap, cap), cap), :],
                dst_ref=arr.at[c, pl.ds(pl.multiple_of(me * cap, cap), cap), :],
                send_sem=send_sem.at[c],
                recv_sem=recv_sem.at[c],
                device_id={"rows": peer},
                device_id_type=MESH,
            ).start()

    ahead = 2

    @pl.loop(0, chunks)
    def _(c):
        fill(c)

        @pl.when(c < ahead)
        def _():
            send(c)

    def landed(ref, sem):
        pltpu.make_async_copy(ref, ref, sem).wait()

    others = owners - 1
    landed(ids_in.at[0:others], ids_sem.at[1])
    landed(ids_out.at[0:others], ids_sem.at[0])

    codes = ids_in[...].reshape(owners, 1, LANES)
    spread = jnp.broadcast_to(codes, (owners, cap, LANES)).reshape(slots, LANES)
    lane = lax.broadcasted_iota(I32, (slots, LANES), 1)
    place = lax.broadcasted_iota(I32, (slots, LANES), 0) % cap
    id_col = jnp.sum(jnp.where(lane == place, spread, 0).astype(F32), axis=1, keepdims=True) - 1.0
    id_wide = jnp.broadcast_to(id_col, (slots, LANES))
    id_row = id_wide.T[0:1, :].astype(I32)
    id_col = id_col.astype(I32)
    for b in range(slots // block):
        k = lax.broadcasted_iota(I32, (block, per_owner), 1)
        pick[b * block : (b + 1) * block, :] = bf(k == id_col[b * block : (b + 1) * block, :])
    for b in range(per_owner // block):
        k = lax.broadcasted_iota(I32, (block, slots), 0) + b * block
        pick_t[b * block : (b + 1) * block, :] = bf(k == id_row)

    cnt[0] = jnp.dot(jnp.ones((8, slots), BF16), pick[...], preferred_element_type=F32)
    for d, mate in enumerate(mates):
        pltpu.make_async_remote_copy(
            src_ref=cnt.at[0], dst_ref=cnt.at[d + 1], send_sem=cnt_sem.at[0], recv_sem=cnt_sem.at[1],
            device_id={"rep": mate}, device_id_type=MESH,
        ).start()
    landed(cnt.at[1:copies], cnt_sem.at[1])
    landed(cnt.at[1:copies], cnt_sem.at[0])
    prior_row = prior_ref[...].astype(F32)
    counts = cnt[0, 0:1, :]
    for d in range(1, copies):
        counts += cnt[d, 0:1, :]
    total_row = prior_row + counts
    total_b[...] = jnp.broadcast_to(total_row, (LANES, per_owner)).T
    prior_b[...] = jnp.broadcast_to(prior_row, (LANES, per_owner)).T
    weight_row = jnp.broadcast_to((1.0 / total_row).astype(BF16), (LANES, per_owner))
    weight_b[...] = lax.dot_general(pick[...], weight_row, NT, preferred_element_type=F32)
    sumsq[...] = jnp.zeros_like(sumsq)
    acc[...] = jnp.zeros_like(acc)
    old_copy.wait()

    def quarter_of(q):
        return pl.ds(pl.multiple_of(q * quarter, quarter), quarter)

    def scatter(c):
        for d, mate in enumerate(mates):
            pltpu.make_async_remote_copy(
                src_ref=part.at[c, quarter_of(mate), :],
                dst_ref=rs_in.at[c, d],
                send_sem=rs_sem.at[0, c], recv_sem=rs_sem.at[1, c],
                device_id={"rep": mate}, device_id_type=MESH,
            ).start()

    def gather(c):
        landed(rs_in.at[c], rs_sem.at[1, c])
        own = quarter_of(rep)
        sums = part[c, own, :]
        for d in range(copies - 1):
            sums += rs_in[c, d]
        cols = pl.ds(pl.multiple_of(c * wide, wide), wide)
        was = old[own, cols].astype(F32)
        mean[c, own, :] = (prior_b[own, :] * was + sums) / total_b[own, :]
        for mate in mates:
            pltpu.make_async_remote_copy(
                src_ref=mean.at[c, own, :],
                dst_ref=mean.at[c, own, :],
                send_sem=ag_sem.at[0, c], recv_sem=ag_sem.at[1, c],
                device_id={"rep": mate}, device_id_type=MESH,
            ).start()

    def square(c):
        landed(rs_in.at[c], ag_sem.at[1, c])
        m = mean[c]
        sumsq[...] += m * m

    @pl.loop(0, chunks)
    def _(c):
        landed(arr.at[c, 0 : others * cap, :], recv_sem.at[c])

        @pl.when(c + ahead < chunks)
        def _():
            send(c + ahead)

        part[c] = jnp.dot(pick_t[...], arr[c], preferred_element_type=F32)
        scatter(c)

        @pl.when(c >= 1)
        def _():
            gather(c - 1)

        @pl.when(c >= 2)
        def _():
            square(c - 2)

    gather(chunks - 1)
    square(chunks - 2)
    square(chunks - 1)

    norm = jnp.sum(sumsq[...], axis=1, keepdims=True) + 1e-06
    sumsq[...] = jnp.broadcast_to(lax.rsqrt(norm), (per_owner, LANES))

    pair = 2

    @pl.loop(0, chunks // pair)
    def _(g):
        cols = pl.ds(pl.multiple_of(g * pair * wide, pair * wide), pair * wide)
        scaled = [(mean[g * pair + i] * sumsq[...]).astype(BF16) for i in range(pair)]
        cent_ref[:, cols] = jnp.concatenate(scaled, axis=1)
        near = jnp.dot(pick[...], cent_ref[:, cols], preferred_element_type=F32)
        for i in range(pair):
            diff = arr[g * pair + i].astype(F32) - near[:, i * wide : (i + 1) * wide]
            acc[...] += diff * diff

    dist = jnp.sum(acc[...], axis=1, keepdims=True)
    scores = weight_b[...] * dist
    scores = jnp.where(lane == place, scores, 0.0).reshape(owners, cap, LANES)
    sc_out[...] = jnp.sum(scores, axis=1, keepdims=True)
    sc_in[pl.ds(me, 1)] = sc_out[pl.ds(me, 1)]
    for peer in peers:
        pltpu.make_async_remote_copy(
            src_ref=sc_out.at[pl.ds(peer, 1)],
            dst_ref=sc_in.at[pl.ds(me, 1)],
            send_sem=sc_sem.at[0], recv_sem=sc_sem.at[1],
            device_id={"rows": peer}, device_id_type=MESH,
        ).start()
    landed(sc_in.at[0:others], sc_sem.at[1])
    back = sc_in[...].reshape(owners, LANES)
    mine_f = jnp.where(mine, 1.0, 0.0)
    found = lax.dot_general(
        back, mine_f, TN, precision=lax.Precision.HIGHEST, preferred_element_type=F32
    )
    score_ref[...] = jnp.sum(jnp.where(at_rank, found, 0.0), axis=0, keepdims=True)

    landed(sc_out.at[0:others], sc_sem.at[0])

    @pl.loop(0, chunks)
    def _(c):
        landed(out.at[c, 0 : others * cap, :], send_sem.at[c])
        landed(rs_in.at[c], rs_sem.at[0, c])
        landed(rs_in.at[c], ag_sem.at[0, c])


def on_device(embeddings, assignments, old_centroids, prior_counts):
    rows_here, width = embeddings.shape
    owners, copies = lax.axis_size("rows"), lax.axis_size("rep")
    per_owner = old_centroids.shape[0]
    cap = 2 * rows_here // owners
    slots = owners * cap
    chunks = width // LANES
    wide = LANES
    quarter = per_owner // copies
    vmem = pl.BlockSpec(memory_space=pltpu.VMEM)
    dma = pltpu.SemaphoreType.DMA
    centroids, row_score = pl.pallas_call(
        functools.partial(kernel, owners, copies, cap, chunks),
        out_shape=(
            jax.ShapeDtypeStruct((per_owner, width), BF16),
            jax.ShapeDtypeStruct((1, rows_here), F32),
        ),
        in_specs=[vmem, vmem, pl.BlockSpec(memory_space=pl.ANY), vmem],
        out_specs=(vmem, vmem),
        scratch_shapes=[
            pltpu.VMEM((chunks, slots, wide), BF16),
            pltpu.VMEM((chunks, slots, wide), BF16),
            pltpu.VMEM((slots, per_owner), BF16),
            pltpu.VMEM((per_owner, slots), BF16),
            pltpu.VMEM((chunks, per_owner, wide), F32),
            pltpu.VMEM((chunks, copies - 1, quarter, wide), F32),
            pltpu.VMEM((chunks, per_owner, wide), F32),
            pltpu.VMEM((slots, LANES), F32),
            pltpu.VMEM((per_owner, width), BF16),
            pltpu.VMEM((per_owner, LANES), F32),
            pltpu.VMEM((per_owner, LANES), F32),
            pltpu.VMEM((slots, LANES), F32),
            pltpu.VMEM((per_owner, LANES), F32),
            pltpu.VMEM((owners, 1, LANES), I32),
            pltpu.VMEM((owners, 1, LANES), I32),
            pltpu.VMEM((copies, 8, per_owner), F32),
            pltpu.VMEM((owners, 1, LANES), F32),
            pltpu.VMEM((owners, 1, LANES), F32),
            dma((chunks,)), dma((chunks,)), dma((2,)), dma((2,)),
            dma((2, chunks)), dma((2, chunks)), dma((2,)), dma,
        ],
        compiler_params=pltpu.CompilerParams(
            collective_id=0, has_side_effects=True, vmem_limit_bytes=60 * 2**20
        ),
        name="centroid_step",
    )(embeddings, assignments.reshape(1, rows_here), old_centroids, prior_counts.reshape(1, per_owner))
    return centroids, row_score.reshape(rows_here)


def solution(mesh):
    placed = (P(("rows", "rep"), None), P(("rows", "rep")), P("rows", None), P("rows"))
    return jax.shard_map(
        on_device,
        mesh=mesh,
        in_specs=placed,
        out_specs=(P("rows", None), P(("rows", "rep"))),
        check_vma=False,
    )
```

time: 318 us -> 149 us (0.47)
  Pallas kernels: 0 us -> 145 us
  waiting for transfers between devices: 132 us -> 0 us
  other arithmetic: 58.7 us -> 0 us
  local copies, waits for them, and re-layouts: 60 us -> 3.68 us
  starting transfers between devices: 34.2 us -> 0 us
  between operations: 14.2 us -> 0.65 us
  matrix products: 8.8 us -> 0 us
  blocking collectives: 8.73 us -> 0 us
    pallas_call x0 -> x1, Pallas kernels: none -> 145 us  [on_device(): pl.pallas_call(functools.partial(kernel, owners, copies, cap, chunks), ou...]
    all_to_all x3 -> x0, waiting for transfers between devices: 102 us -> none  [the longest x1 92.9 us: on_device(): lax.all_to_all(outgoing, 'rows', split_axis=0, concat_axis=0, tiled=True)]
    gather x10 -> x0, local copies, waits for them, and re-layouts: 58.5 us -> none  [the longest x1 13.1 us: on_device(): weight[flat_safe].astype(jnp.float32) * dist]
    gather x3 -> x0, other arithmetic: 39.8 us -> none  [the longest x1 39.7 us: on_device(): slot_of = jnp.arange(rows_here, dtype=jnp.int32) - starts[owner_of]]
    all_to_all x3 -> x0, starting transfers between devices: 34.1 us -> none  [the longest x1 13 us: on_device(): lax.all_to_all(local_ids, 'rows', split_axis=0, concat_axis=0, tiled=True)]
    psum x1 -> x0, waiting for transfers between devices: 29.9 us -> none  [on_device(): sums, counts = lax.psum((partial_sums, tally), 'rep')]
    reduce_sum x5 -> x0, other arithmetic: 10.3 us -> none  [the longest x1 4.88 us: on_device(): dist = jnp.sum(diff * diff, axis=1)]
    dot_general x1 -> x0, matrix products: 8.8 us -> none  [on_device(): lax.dot_general(onehot, flat, (((0,), (0,)), ((), ())), preferred_element...]
  transfers between devices with their start and end apart: 4 -> 0, of which waited for: 3 -> 0; matrix products, arithmetic and copies ran while one was open for 23% -> 0% of each run, Pallas kernels for 0% -> 0%
where the time goes in v1:
time: 149 us
  Pallas kernels  145 us (97%)
  local copies, waits for them, and re-layouts  3.68 us (2%)
    pallas_call x1, Pallas kernels, on_device(): pl.pallas_call(functools.partial(kernel, owners, copies, cap, chunks), ou...  145 us
    unnamed x4, local copies, waits for them, and re-layouts  3.68 us

profile of v1, /device:TPU:1, one launch (start us, length us, event | category | flops | bytes accessed | tf_op | source)
XLA Modules:
  0.0 149.3 jit_solution(14402136958317704540)
XLA Ops:
  0.6 145.0 %centroid_step.1 = (bf16[1024,1024]{1,0:T(8,128)(2,1)}, f32[1,1024]{1,0:T(1,128)}) custom-call(bf16[1024,1024]{1,0:T(8,128)(2,1)} %emb_ref.1, s32[1,1024]{1,0:T(1,128)} %bitcast.4, bf16[1024,1024]{1,0:T(8,128)(2,1)} %old_ref.1, s32[1,1024]{1,0:T(1,128)} %bitcast.5), custom_call_target="tpu_custom_call" | custom-call | tf_op jit(solution)/shard_map/centroid_step/pallas_call | solution.py:287
  145.6 0.0 copy-start
  145.6 3.1 %copy.8 = bf16[1024,1024]{1,0:T(8,128)(2,1)} copy(bf16[1024,1024]{1,0:T(8,128)(2,1)} %get-tuple-element.8) | data formatting | bytes 4194304
  148.7 0.0 copy-done
  148.7 0.6 copy.9
Async XLA Ops:
  145.6 3.1 %copy-start = (f32[1,1024]{1,0:T(1,128)S(1)}, f32[1,1024]{1,0:T(1,128)}, u32[]{:S(2)}) copy-start(f32[1,1024]{1,0:T(1,128)} %get-tuple-element.5) | copy-start | bytes 12292

commit v2 on v1

v2 whole, which is shorter than its diff:
```python
import functools

import jax
import jax.numpy as jnp
from jax import lax
from jax.experimental import pallas as pl
from jax.experimental.pallas import tpu as pltpu
from jax.sharding import PartitionSpec as P

MESH = pl.DeviceIdType.MESH
F32, BF16, I32 = jnp.float32, jnp.bfloat16, jnp.int32
LANES = 128
NT = (((1,), (1,)), ((), ()))
TN = (((0,), (0,)), ((), ()))


def displacements(planes, columns):
    z_order = []
    for step in range(planes // 2, 0, -1):
        z_order += [step, planes - step] if step != planes - step else [step]
    half = len(z_order) // 2
    z_order = [z for pair in zip(z_order[:half], z_order[half:]) for z in pair] + z_order[2 * half :]
    z_order.append(0)
    order = [
        (z_order[i % planes], (i // planes + i) % columns, (i // (planes * columns) + i) % 2)
        for i in range(planes * columns * 2)
    ]
    assert len(set(order)) == planes * columns * 2
    return [one for one in order if one != (0, 0, 0)]


def bf(mask):
    return jnp.where(mask, 1.0, 0.0).astype(BF16)


def kernel(
    owners, copies, cap, chunks, late,
    emb_hbm, assign_ref, old_ref, prior_ref,
    cent_ref, score_ref,
    emb, out, arr, pick, pick_t, part, rs_in, mean, cent, acc, old, total_b, prior_b, weight_b,
    sumsq, scale, scale_msg,
    ids_out, ids_in, cnt, sc_out, sc_in,
    send_sem, recv_sem, ids_sem, cnt_sem, rs_sem, ag_sem, scale_sem, sc_sem, old_sem, emb_sem,
    cent_sem,
):
    rows_here, width = emb.shape
    per_owner = old.shape[0]
    slots = owners * cap
    wide = width // chunks
    quarter = per_owner // copies
    me, rep = lax.axis_index("rows"), lax.axis_index("rep")
    columns = 4
    planes = owners // (2 * columns)
    z, x, core = me // (2 * columns), (me // 2) % columns, me % 2
    peers = [
        ((z + dz) % planes) * (2 * columns) + ((x + dx) % columns) * 2 + (core + dc) % 2
        for dz, dx, dc in displacements(planes, columns)
    ]
    mates = [lax.rem(rep + d, copies) for d in range(1, copies)]
    others = owners - 1

    emb_copy = pltpu.make_async_copy(emb_hbm, emb, emb_sem)
    emb_copy.start()

    barrier = pltpu.get_barrier_semaphore()
    for peer in peers:
        pl.semaphore_signal(barrier, inc=1, device_id={"rows": peer}, device_id_type=MESH)
    for mate in mates:
        pl.semaphore_signal(barrier, inc=1, device_id={"rep": mate}, device_id_type=MESH)

    old_copy = pltpu.make_async_copy(old_ref, old, old_sem)
    old_copy.start()

    def landed(ref, sem):
        pltpu.make_async_copy(ref, ref, sem).wait()

    def tell(src, dst, sems, **where):
        pltpu.make_async_remote_copy(
            src_ref=src, dst_ref=dst, send_sem=sems[0], recv_sem=sems[1],
            device_id=where, device_id_type=MESH,
        ).start()

    def columns_of(c, n=1):
        return pl.ds(pl.multiple_of(c * wide, wide), n * wide)

    def slots_of(owner):
        return pl.ds(pl.multiple_of(owner * cap, cap), cap)

    def quarter_of(q):
        return pl.ds(pl.multiple_of(q * quarter, quarter), quarter)

    assign = assign_ref[...]
    owner_row = assign // per_owner
    local_row = assign - owner_row * per_owner
    owner_col = lax.broadcasted_iota(I32, (owners, rows_here), 0)
    mine = owner_row == owner_col
    starts = jnp.sum(jnp.where(owner_row < owner_col, 1.0, 0.0), axis=1, keepdims=True)
    start_row = jnp.sum(jnp.where(mine, starts, 0.0), axis=0, keepdims=True).astype(I32)
    rank_row = lax.broadcasted_iota(I32, (1, rows_here), 1) - start_row
    slot_row = owner_row * cap + rank_row

    block = 256
    for b in range(slots // block):
        s = lax.broadcasted_iota(I32, (block, rows_here), 0) + b * block
        pick[b * block : (b + 1) * block, :] = bf(s == slot_row)

    def fill(c):
        out[c] = jnp.dot(pick[...], emb[:, columns_of(c)], preferred_element_type=F32).astype(BF16)
        arr[c, slots_of(me), :] = out[c, slots_of(me), :]

    def send(c):
        for peer in peers:
            tell(
                out.at[c, slots_of(peer), :], arr.at[c, slots_of(me), :],
                (send_sem.at[c], recv_sem.at[c]), rows=peer,
            )

    emb_copy.wait()
    fill(0)
    pl.semaphore_wait(barrier, len(peers) + len(mates))
    send(0)

    code = local_row + 1
    at_rank = lax.broadcasted_iota(I32, (LANES, rows_here), 0) == rank_row
    high = jnp.where(at_rank, code // 32, 0).astype(F32).astype(BF16)
    low = jnp.where(at_rank, code % 32, 0).astype(F32).astype(BF16)
    mine_b = bf(mine)
    code_out = 32.0 * lax.dot_general(mine_b, high, NT, preferred_element_type=F32)
    code_out += lax.dot_general(mine_b, low, NT, preferred_element_type=F32)
    ids_out[...] = code_out.astype(I32).reshape(owners, 1, LANES)
    ids_in[pl.ds(me, 1)] = ids_out[pl.ds(me, 1)]
    for peer in peers:
        tell(ids_out.at[pl.ds(peer, 1)], ids_in.at[pl.ds(me, 1)], (ids_sem.at[0], ids_sem.at[1]), rows=peer)

    ahead = 3

    @pl.loop(1, chunks)
    def _(c):
        fill(c)

        @pl.when(c < ahead)
        def _():
            send(c)

    landed(ids_in.at[0:others], ids_sem.at[1])
    landed(ids_out.at[0:others], ids_sem.at[0])

    codes = ids_in[...].reshape(owners, 1, LANES)
    spread = jnp.broadcast_to(codes, (owners, cap, LANES)).reshape(slots, LANES)
    lane = lax.broadcasted_iota(I32, (slots, LANES), 1)
    place = lax.broadcasted_iota(I32, (slots, LANES), 0) % cap
    id_col = jnp.sum(jnp.where(lane == place, spread, 0).astype(F32), axis=1, keepdims=True) - 1.0
    id_wide = jnp.broadcast_to(id_col, (slots, LANES))
    id_row = id_wide.T[0:1, :].astype(I32)
    id_col = id_col.astype(I32)
    for b in range(slots // block):
        k = lax.broadcasted_iota(I32, (block, per_owner), 1)
        pick[b * block : (b + 1) * block, :] = bf(k == id_col[b * block : (b + 1) * block, :])
    for b in range(per_owner // block):
        k = lax.broadcasted_iota(I32, (block, slots), 0) + b * block
        pick_t[b * block : (b + 1) * block, :] = bf(k == id_row)

    cnt[0] = jnp.dot(jnp.ones((8, slots), BF16), pick[...], preferred_element_type=F32)
    for d, mate in enumerate(mates):
        tell(cnt.at[0], cnt.at[d + 1], (cnt_sem.at[0], cnt_sem.at[1]), rep=mate)
    landed(cnt.at[1:copies], cnt_sem.at[1])
    landed(cnt.at[1:copies], cnt_sem.at[0])
    prior_row = prior_ref[...].astype(F32)
    counts = cnt[0, 0:1, :]
    for d in range(1, copies):
        counts += cnt[d, 0:1, :]
    total_row = prior_row + counts
    total_b[...] = jnp.broadcast_to(total_row, (LANES, per_owner)).T
    prior_b[...] = jnp.broadcast_to(prior_row, (LANES, per_owner)).T
    weight_row = jnp.broadcast_to((1.0 / total_row).astype(BF16), (LANES, per_owner))
    weight_b[...] = lax.dot_general(pick[...], weight_row, NT, preferred_element_type=F32)
    sumsq[...] = jnp.zeros_like(sumsq)
    acc[...] = jnp.zeros_like(acc)
    old_copy.wait()
    own = quarter_of(rep)

    def partial(c, q):
        part[c, quarter_of(q), :] = jnp.dot(
            pick_t[quarter_of(q), :], arr[c], preferred_element_type=F32
        )

    def settle(c):
        landed(rs_in.at[c], rs_sem.at[1, c])
        sums = part[c, own, :]
        for d in range(copies - 1):
            sums += rs_in[c, d]
        was = old[own, columns_of(c)].astype(F32)
        here = (prior_b[own, :] * was + sums) / total_b[own, :]
        mean[c, own, :] = here
        sumsq[...] += here * here

    def share(c):
        for mate in mates:
            tell(mean.at[c, own, :], mean.at[c, own, :], (ag_sem.at[0, c], ag_sem.at[1, c]), rep=mate)

    @pl.loop(0, chunks)
    def _(c):
        landed(arr.at[c, 0 : others * cap, :], recv_sem.at[c])

        @pl.when(c + ahead < chunks)
        def _():
            send(c + ahead)

        for d in (1, 0, 2):
            partial(c, mates[d])
            tell(
                part.at[c, quarter_of(mates[d]), :], rs_in.at[c, d],
                (rs_sem.at[0, c], rs_sem.at[1, c]), rep=mates[d],
            )
        partial(c, rep)

        @pl.when(c >= 1)
        def _():
            settle(c - 1)

        @pl.when(jnp.logical_and(c >= 1, c <= chunks - late))
        def _():
            share(c - 1)

    settle(chunks - 1)
    norm = jnp.sum(sumsq[...], axis=1, keepdims=True) + 1e-06
    scale_own = jnp.broadcast_to(lax.rsqrt(norm), (quarter, LANES))
    scale_msg[rep] = scale_own.T[0:8, :]
    for mate in mates:
        tell(scale_msg.at[rep], scale_msg.at[rep], (scale_sem.at[0], scale_sem.at[1]), rep=mate)
    for c in range(chunks - late, chunks):
        cent[c, own, :] = (mean[c, own, :] * scale_own).astype(BF16)
        for mate in mates:
            tell(cent.at[c, own, :], cent.at[c, own, :], (ag_sem.at[0, c], ag_sem.at[1, c]), rep=mate)
    landed(scale_msg.at[0 : copies - 1], scale_sem.at[1])
    for q in range(copies):
        scale[q * quarter : (q + 1) * quarter, :] = jnp.broadcast_to(
            scale_msg[q, 0:1, :], (LANES, quarter)
        ).T

    def write_out(c):
        return pltpu.make_async_copy(cent.at[c], cent_ref.at[:, columns_of(c)], cent_sem.at[c])

    def finish(c):
        landed(rs_in.at[c], ag_sem.at[1, c])
        cent[c] = (mean[c] * scale[...]).astype(BF16)
        write_out(c).start()

    def both(c):
        return jnp.concatenate([cent[c], cent[c + 1]], axis=1)

    def gap(c, where, near):
        one = arr[c, where, :].astype(F32) - near[:, 0:wide]
        two = arr[c + 1, where, :].astype(F32) - near[:, wide:]
        return one * one + two * two

    @pl.loop(0, chunks // 2 - 1)
    def _(g):
        finish(2 * g)
        finish(2 * g + 1)
        near = jnp.dot(pick[...], both(2 * g), preferred_element_type=F32)
        acc[...] += gap(2 * g, slice(None), near)

    for c in range(chunks - 2, chunks):
        if c < chunks - late:
            finish(c)
        else:
            landed(cent.at[c, 0 : per_owner - quarter, :], ag_sem.at[1, c])
            write_out(c).start()

    groups = 4
    held = owners // groups
    span = held * cap
    here_lane = lax.broadcasted_iota(I32, (span, LANES), 1)
    here_place = lax.broadcasted_iota(I32, (span, LANES), 0) % cap
    sc_sems = (sc_sem.at[0], sc_sem.at[1])
    for turn in (2, 1, 3, 0):
        first = lax.rem(me // held + turn, groups) * held
        where = pl.ds(pl.multiple_of(first * cap, span), span)
        near = jnp.dot(pick[where, :], both(chunks - 2), preferred_element_type=F32)
        dist = jnp.sum(acc[where, :] + gap(chunks - 2, where, near), axis=1, keepdims=True)
        scores = weight_b[where, :] * dist
        scores = jnp.where(here_lane == here_place, scores, 0.0).reshape(held, cap, LANES)
        sc_out[pl.ds(first, held)] = jnp.sum(scores, axis=1, keepdims=True)
        for j in range(1 if turn == 0 else 0, held):
            peer = first + (lax.rem(me + j, held) if turn == 0 else j)
            tell(sc_out.at[pl.ds(peer, 1)], sc_in.at[pl.ds(me, 1)], sc_sems, rows=peer)
    sc_in[pl.ds(me, 1)] = sc_out[pl.ds(me, 1)]

    @pl.loop(0, chunks)
    def _(c):
        landed(out.at[c, 0 : others * cap, :], send_sem.at[c])
        landed(rs_in.at[c], rs_sem.at[0, c])
        write_out(c).wait()

    for c in range(chunks):
        if c < chunks - late:
            landed(rs_in.at[c], ag_sem.at[0, c])
        else:
            landed(cent.at[c, 0 : per_owner - quarter, :], ag_sem.at[0, c])
    landed(scale_msg.at[0 : copies - 1], scale_sem.at[0])

    landed(sc_in.at[0:others], sc_sem.at[1])
    back = sc_in[...].reshape(owners, LANES)
    found = lax.dot_general(
        back, jnp.where(mine, 1.0, 0.0), TN, precision=lax.Precision.HIGHEST, preferred_element_type=F32
    )
    score_ref[...] = jnp.sum(jnp.where(at_rank, found, 0.0), axis=0, keepdims=True)
    landed(sc_out.at[0:others], sc_sem.at[0])


def on_device(embeddings, assignments, old_centroids, prior_counts):
    rows_here, width = embeddings.shape
    owners, copies = lax.axis_size("rows"), lax.axis_size("rep")
    per_owner = old_centroids.shape[0]
    cap = 2 * rows_here // owners
    slots = owners * cap
    chunks = width // LANES
    wide = LANES
    quarter = per_owner // copies
    late = 2
    vmem = pl.BlockSpec(memory_space=pltpu.VMEM)
    dma = pltpu.SemaphoreType.DMA
    anywhere = pl.BlockSpec(memory_space=pl.ANY)
    centroids, row_score = pl.pallas_call(
        functools.partial(kernel, owners, copies, cap, chunks, late),
        out_shape=(
            jax.ShapeDtypeStruct((per_owner, width), BF16),
            jax.ShapeDtypeStruct((1, rows_here), F32),
        ),
        in_specs=[anywhere, vmem, anywhere, vmem],
        out_specs=(anywhere, vmem),
        scratch_shapes=[
            pltpu.VMEM((rows_here, width), BF16),
            pltpu.VMEM((chunks, slots, wide), BF16),
            pltpu.VMEM((chunks, slots, wide), BF16),
            pltpu.VMEM((slots, per_owner), BF16),
            pltpu.VMEM((per_owner, slots), BF16),
            pltpu.VMEM((chunks, per_owner, wide), F32),
            pltpu.VMEM((chunks, copies - 1, quarter, wide), F32),
            pltpu.VMEM((chunks, per_owner, wide), F32),
            pltpu.VMEM((chunks, per_owner, wide), BF16),
            pltpu.VMEM((slots, LANES), F32),
            pltpu.VMEM((per_owner, width), BF16),
            pltpu.VMEM((per_owner, LANES), F32),
            pltpu.VMEM((per_owner, LANES), F32),
            pltpu.VMEM((slots, LANES), F32),
            pltpu.VMEM((quarter, LANES), F32),
            pltpu.VMEM((per_owner, LANES), F32),
            pltpu.VMEM((copies, 8, quarter), F32),
            pltpu.VMEM((owners, 1, LANES), I32),
            pltpu.VMEM((owners, 1, LANES), I32),
            pltpu.VMEM((copies, 8, per_owner), F32),
            pltpu.VMEM((owners, 1, LANES), F32),
            pltpu.VMEM((owners, 1, LANES), F32),
            dma((chunks,)), dma((chunks,)), dma((2,)), dma((2,)),
            dma((2, chunks)), dma((2, chunks)), dma((2,)), dma((2,)), dma, dma, dma((chunks,)),
        ],
        compiler_params=pltpu.CompilerParams(
            collective_id=0, has_side_effects=True, vmem_limit_bytes=46 * 2**20
        ),
        name="centroid_step",
    )(*[
        pltpu.with_memory_space_constraint(one, pltpu.HBM)
        for one in (
            embeddings, assignments.reshape(1, rows_here), old_centroids,
            prior_counts.reshape(1, per_owner),
        )
    ])
    return centroids, row_score.reshape(rows_here)


def solution(mesh):
    placed = (P(("rows", "rep"), None), P(("rows", "rep")), P("rows", None), P("rows"))
    return jax.shard_map(
        on_device,
        mesh=mesh,
        in_specs=placed,
        out_specs=(P("rows", None), P(("rows", "rep"))),
        check_vma=False,
    )
```

time: 149 us -> 139 us (0.933)
  Pallas kernels: 145 us -> 136 us
  local copies, waits for them, and re-layouts: 3.68 us -> 1.91 us
    pallas_call x1, Pallas kernels: 145 us -> 136 us  [on_device(): pl.pallas_call(functools.partial(kernel, owners, copies, cap, chunks, lat...]
    unnamed x4 -> x2, local copies, waits for them, and re-layouts: 3.68 us -> 1.91 us
where the time goes in v2:
time: 139 us; the launch traced here: 138 us
  Pallas kernels  136 us (98%)
  local copies, waits for them, and re-layouts  1.91 us (1%)
    pallas_call x1, Pallas kernels, on_device(): pl.pallas_call(functools.partial(kernel, owners, copies, cap, chunks, lat...  136 us

profile of v2, /device:TPU:1, one launch (start us, length us, event | category | flops | bytes accessed | tf_op | source)
XLA Modules:
  0.0 138.4 jit_solution(12733706933860984194)
XLA Ops:
  0.6 135.8 %centroid_step.1 = (bf16[1024,1024]{1,0:T(8,128)(2,1)S(1)}, f32[1,1024]{1,0:T(1,128)S(1)}) custom-call(bf16[1024,1024]{1,0:T(8,128)(2,1)} %emb_hbm.1, s32[1,1024]{1,0:T(1,128)} %bitcast.4, bf16[1024,1024]{1,0:T(8,128)(2,1)} %old_ref.1, s32[1,1024]{1,0:T(1,128)} %bitcast.5), custom_call_target="tpu_custom_call" | custom-call | tf_op jit(solution)/shard_map/centroid_step/pallas_call | solution.py:325
  136.5 1.3 copy.8
  137.8 0.6 copy.9

commit v3 on v2

--- a/solution.py
+++ b/solution.py
@@ -230,7 +230,7 @@
         tell(scale_msg.at[rep], scale_msg.at[rep], (scale_sem.at[0], scale_sem.at[1]), rep=mate)
     for c in range(chunks - late, chunks):
         cent[c, own, :] = (mean[c, own, :] * scale_own).astype(BF16)
-        for mate in mates:
+        for mate in (mates[1], mates[0], mates[2]):
             tell(cent.at[c, own, :], cent.at[c, own, :], (ag_sem.at[0, c], ag_sem.at[1, c]), rep=mate)
     landed(scale_msg.at[0 : copies - 1], scale_sem.at[1])
     for q in range(copies):
@@ -261,12 +261,16 @@
         near = jnp.dot(pick[...], both(2 * g), preferred_element_type=F32)
         acc[...] += gap(2 * g, slice(None), near)
 
+    def single(c, where):
+        near = jnp.dot(pick[where, :], cent[c], preferred_element_type=F32)
+        diff = arr[c, where, :].astype(F32) - near
+        return diff * diff
+
     for c in range(chunks - 2, chunks):
-        if c < chunks - late:
-            finish(c)
-        else:
-            landed(cent.at[c, 0 : per_owner - quarter, :], ag_sem.at[1, c])
-            write_out(c).start()
+        landed(cent.at[c, 0 : per_owner - quarter, :], ag_sem.at[1, c])
+        write_out(c).start()
+        if c < chunks - 1:
+            acc[...] += single(c, slice(None))
 
     groups = 4
     held = owners // groups
@@ -277,8 +281,7 @@
     for turn in (2, 1, 3, 0):
         first = lax.rem(me // held + turn, groups) * held
         where = pl.ds(pl.multiple_of(first * cap, span), span)
-        near = jnp.dot(pick[where, :], both(chunks - 2), preferred_element_type=F32)
-        dist = jnp.sum(acc[where, :] + gap(chunks - 2, where, near), axis=1, keepdims=True)
+        dist = jnp.sum(acc[where, :] + single(chunks - 1, where), axis=1, keepdims=True)
         scores = weight_b[where, :] * dist
         scores = jnp.where(here_lane == here_place, scores, 0.0).reshape(held, cap, LANES)
         sc_out[pl.ds(first, held)] = jnp.sum(scores, axis=1, keepdims=True)

time: 139 us -> 142 us (1.022)
  Pallas kernels: 136 us -> 140 us
    pallas_call x1, Pallas kernels: 136 us -> 140 us  [on_device(): pl.pallas_call(functools.partial(kernel, owners, copies, cap, chunks, lat...]
where the time goes in v3:
time: 142 us
  Pallas kernels  140 us (99%)
  local copies, waits for them, and re-layouts  1.91 us (1%)
    pallas_call x1, Pallas kernels, on_device(): pl.pallas_call(functools.partial(kernel, owners, copies, cap, chunks, lat...  140 us

profile of v3, /device:TPU:1, one launch (start us, length us, event | category | flops | bytes accessed | tf_op | source)
XLA Modules:
  0.0 142.2 jit_solution(745257095361666349)
XLA Ops:
  0.6 139.6 %centroid_step.1 = (bf16[1024,1024]{1,0:T(8,128)(2,1)S(1)}, f32[1,1024]{1,0:T(1,128)S(1)}) custom-call(bf16[1024,1024]{1,0:T(8,128)(2,1)} %emb_hbm.1, s32[1,1024]{1,0:T(1,128)} %bitcast.4, bf16[1024,1024]{1,0:T(8,128)(2,1)} %old_ref.1, s32[1,1024]{1,0:T(1,128)} %bitcast.5), custom_call_target="tpu_custom_call" | custom-call | tf_op jit(solution)/shard_map/centroid_step/pallas_call | solution.py:328
  140.3 1.3 copy.8
  141.6 0.6 copy.9
